TPU v7x, 256 devices: a whole 4x4x8 slice. The times are simulated.
256 devices in a mesh: cfg: 2 (over core), req: 4 (over y), seq: 32 (over z, x).
Axes of the slice: x: 4, y: 4, z: 8, core: 2. Of those that a mesh axis runs over, the one named last changes fastest.
Arguments:
- patches: float32 [16, 1024, 16], P('req', 'seq'), may hold values from -6 to 6
- noise: float32 [16, 1024, 16], P('req', 'seq'), may hold values from -6 to 6
- timesteps: int32 [16], replicated, may hold values from 50 to 950
- labels: int32 [16], replicated, may hold values from 0 to 999
- lengths: int32 [16], replicated, may hold values from 1 to 1024, 12288 in all
- time_w1: bfloat16 [256, 1152], replicated, may hold values from -0.375 to 0.375
- time_w2: bfloat16 [1152, 1152], replicated, may hold values from -0.1875 to 0.1875
- label_table: bfloat16 [1001, 1152], replicated, may hold values from -5 to 5
- patch_w: bfloat16 [16, 1152], replicated, may hold values from -1.5 to 1.5
- mod_w: bfloat16 [1152, 5760], P(None, ('req', 'seq')), may hold values from -0.1875 to 0.1875
- qkv_w: bfloat16 [1152, 3456], P('req')
- out_w: bfloat16 [1152, 1152], P(None, 'req'), may hold values from -0.1875 to 0.1875
- head_w: bfloat16 [1152, 32], replicated, may hold values from -0.1875 to 0.1875
Outputs:
- guided_update: float32 [16, 1024, 16], P('req', 'seq', 'cfg')
- hidden_norms: float32 [2, 16], P('cfg', 'req')
- max_logits: float32 [2, 16, 16], P('cfg', 'req')
Inputs may be any that keep to these rules, and one draw needn't show every extreme that they name: The lengths of the 16 requests sum to 12288, and the longest has exactly 1024 tokens.
All inputs are finite; a program needn't handle non-finite values.
Results may differ from a plain program's by a relative error of at most 0.0029.
Values may be sent and summed in bfloat16 or wider, within the bound.
A program may use at most 128 MiB of HBM per device.

v0:
```python
import math
import jax
import jax.numpy as jnp
from jax import lax
from jax.sharding import PartitionSpec as P

HEADS = 16
FREQ = 256
norm_eps = 1e-06
masked_score = -1e30
guide_scale = 4.0
plan_offset = 0.008
diffusion_steps = 1000.0


def partner(value, axis, stride):
    mask = 2**stride
    pairs = [(source, source ^ mask) for source in range(lax.axis_size(axis))]
    return lax.ppermute(value, axis, pairs)


def layer_norm(values):
    center = values - jnp.mean(values, axis=-1, keepdims=True)
    spread = jnp.mean(center * center, axis=-1, keepdims=True)
    return center * lax.rsqrt(spread + norm_eps)


def sine_table(places, count, cos_first):
    half = count // 2
    rates = jnp.exp(-math.log(10000.0) * jnp.arange(half, dtype=jnp.float32) / half)
    angles = places.astype(jnp.float32)[:, None] * rates[None, :]
    if cos_first:
        return jnp.concatenate([jnp.cos(angles), jnp.sin(angles)], axis=1)
    return jnp.concatenate([jnp.sin(angles), jnp.cos(angles)], axis=1)


def alpha_bar(steps):
    phase = (steps / diffusion_steps + plan_offset) / (1.0 + plan_offset) * (math.pi / 2.0)
    return jnp.cos(phase) ** 2


def sampler_step(patches, noise, guided, varpart, steps, valid):
    abar = alpha_bar(steps)
    abar_prev = alpha_bar(steps - 1.0)
    beta = 1.0 - abar / abar_prev
    start = (patches - jnp.sqrt(1.0 - abar) * guided) / jnp.sqrt(abar)
    mean = (
        beta * jnp.sqrt(abar_prev) / (1.0 - abar) * start
        + (1.0 - abar_prev) * jnp.sqrt(1.0 - beta) / (1.0 - abar) * patches
    )
    tilde = beta * (1.0 - abar_prev) / (1.0 - abar)
    frac = (varpart + 1.0) * 0.5
    logvar = frac * jnp.log(beta) + (1.0 - frac) * jnp.log(tilde)
    return jnp.where(valid, mean + jnp.exp(0.5 * logvar) * noise, 0.0)


def body(
    patches,
    noise,
    timesteps,
    labels,
    lengths,
    time_w1,
    time_w2,
    label_table,
    patch_w,
    mod_w,
    qkv_w,
    out_w,
    head_w,
):
    req_dev, slot_dev, patch_in = patches.shape
    width = patch_w.shape[1]
    head_dim = width // HEADS
    seq_total = slot_dev * lax.axis_size("seq")
    copy_index = lax.axis_index("cfg")
    is_cond = copy_index == 0
    tfreq = sine_table(timesteps, FREQ, True).astype(jnp.bfloat16)
    time_hidden = jax.nn.silu(jnp.dot(tfreq, time_w1, preferred_element_type=jnp.float32)).astype(
        jnp.bfloat16
    )
    time_embed = jnp.dot(time_hidden, time_w2, preferred_element_type=jnp.float32)
    label_rows = label_table.shape[0]
    label_used = jnp.where(is_cond, labels, label_rows - 1)
    one_hot = (label_used[:, None] == jnp.arange(label_rows, dtype=jnp.int32)[None, :]).astype(
        jnp.bfloat16
    )
    cond = time_embed + jnp.dot(one_hot, label_table, preferred_element_type=jnp.float32)
    cond_act = jax.nn.silu(cond).astype(jnp.bfloat16)
    mod_part = jnp.dot(cond_act, mod_w, preferred_element_type=jnp.float32)
    mod_all = lax.all_gather(mod_part, ("req", "seq"), axis=1, tiled=True)
    first_req = lax.axis_index("req") * req_dev
    modulation = lax.dynamic_slice_in_dim(mod_all, first_req, req_dev, 0).reshape(req_dev, 5, width)
    my_lengths = lax.dynamic_slice_in_dim(lengths, first_req, req_dev, 0)
    my_steps = lax.dynamic_slice_in_dim(timesteps, first_req, req_dev, 0)
    shift1 = modulation[:, 0][:, None, :]
    scale1 = modulation[:, 1][:, None, :]
    gate1 = modulation[:, 2][:, None, :]
    shift2 = modulation[:, 3][:, None, :]
    scale2 = modulation[:, 4][:, None, :]
    slot_pos = lax.axis_index("seq") * slot_dev + jnp.arange(slot_dev, dtype=jnp.int32)
    position = sine_table(slot_pos, width, False)
    token_rows = req_dev * slot_dev
    embedded = jnp.dot(
        patches.astype(jnp.bfloat16).reshape(token_rows, patch_in),
        patch_w,
        preferred_element_type=jnp.float32,
    )
    hidden0 = embedded.reshape(req_dev, slot_dev, width) + position[None, :, :]
    normed1 = (layer_norm(hidden0) * (1.0 + scale1) + shift1).astype(jnp.bfloat16)
    normed_rows = normed1.reshape(token_rows, width)
    projected = jnp.dot(
        normed_rows,
        lax.all_gather(qkv_w, "req", axis=0, tiled=True),
        preferred_element_type=jnp.float32,
    )
    query = projected[:, :width].astype(jnp.bfloat16).reshape(req_dev, slot_dev, HEADS, head_dim)
    keys_local = (
        projected[:, width : 2 * width].astype(jnp.bfloat16).reshape(req_dev, slot_dev, width)
    )
    values_local = projected[:, 2 * width :].astype(jnp.bfloat16).reshape(req_dev, slot_dev, width)
    inv_root = 1.0 / math.sqrt(head_dim)
    keys_all, values_all = (
        lax.all_gather(keys_local, "seq", axis=1, tiled=True),
        lax.all_gather(values_local, "seq", axis=1, tiled=True),
    )
    keys_heads = keys_all.reshape(req_dev, seq_total, HEADS, head_dim)
    values_heads = values_all.reshape(req_dev, seq_total, HEADS, head_dim)
    scores = (
        jnp.einsum("rqhd,rkhd->rhqk", query, keys_heads, preferred_element_type=jnp.float32)
        * inv_root
    )
    key_ok = (jnp.arange(seq_total, dtype=jnp.int32)[None, :] < my_lengths[:, None])[
        :, None, None, :
    ]
    scores = jnp.where(key_ok, scores, masked_score)
    row_max = jnp.max(scores, axis=3)
    expo = jnp.where(key_ok, jnp.exp(scores - row_max[..., None]), 0.0)
    total = jnp.sum(expo, axis=3)
    summed = jnp.einsum(
        "rhqk,rkhd->rqhd",
        expo.astype(jnp.bfloat16),
        values_heads,
        preferred_element_type=jnp.float32,
    )
    mixed = (
        (summed / jnp.transpose(total, (0, 2, 1))[..., None])
        .astype(jnp.bfloat16)
        .reshape(token_rows, width)
    )
    attended = jnp.dot(
        mixed, lax.all_gather(out_w, "req", axis=1, tiled=True), preferred_element_type=jnp.float32
    )
    hidden1 = hidden0 + gate1 * attended.reshape(req_dev, slot_dev, width)
    query_ok = slot_pos[None, :] < my_lengths[:, None]
    squares = jnp.sum(jnp.where(query_ok[:, :, None], hidden1 * hidden1, 0.0), axis=(1, 2))
    local_top = jnp.max(jnp.where(query_ok[:, None, :], row_max, masked_score), axis=2)
    total_squares = lax.psum(squares, "seq")
    top = lax.pmax(local_top, "seq")
    norm_values = jnp.sqrt(total_squares / (my_lengths.astype(jnp.float32) * width))
    normed2 = (layer_norm(hidden1) * (1.0 + scale2) + shift2).astype(jnp.bfloat16)
    prediction = jnp.dot(
        normed2.reshape(token_rows, width), head_w, preferred_element_type=jnp.float32
    ).reshape(req_dev, slot_dev, head_w.shape[1])
    other = partner(prediction, "cfg", 0)
    pred_cond = jnp.where(is_cond, prediction, other)
    pred_uncond = jnp.where(is_cond, other, prediction)
    eps_cond = pred_cond[..., :patch_in]
    eps_uncond = pred_uncond[..., :patch_in]
    guided = eps_uncond + guide_scale * (eps_cond - eps_uncond)
    varpart = pred_cond[..., patch_in:]
    channel_half = patch_in // lax.axis_size("cfg")
    channel_first = copy_index * channel_half

    def own_channels(values):
        return lax.dynamic_slice_in_dim(values, channel_first, channel_half, 2)

    steps = my_steps.astype(jnp.float32)[:, None, None]
    guided_update = sampler_step(
        own_channels(patches),
        own_channels(noise),
        own_channels(guided),
        own_channels(varpart),
        steps,
        query_ok[:, :, None],
    )
    return (guided_update, norm_values[None, :], top[None, :, :])


def solution(mesh):
    in_specs = (
        P("req", "seq", None),
        P("req", "seq", None),
        P(),
        P(),
        P(),
        P(),
        P(),
        P(),
        P(),
        P(None, ("req", "seq")),
        P("req", None),
        P(None, "req"),
        P(),
    )
    out_specs = (P("req", "seq", "cfg"), P("cfg", "req"), P("cfg", "req", None))
    return jax.shard_map(body, mesh=mesh, in_specs=in_specs, out_specs=out_specs, check_vma=False)
```

profile of v0, /device:TPU:2, one launch (start us, length us, event | category | flops | bytes accessed | tf_op | source)
XLA Modules:
  0.0 769.9 jit_solution(16310428311648811346)
XLA Ops:
  7.2 0.7 all-gather.6.cloned.1.call-update
  8.0 0.7 convert_element_type.45
  8.7 0.7 broadcast_select_fusion.1
  9.5 1.7 fusion.27
  11.1 2.3 convolution_bitcast_fusion
  13.4 348.6 %all-gather = f32[128,45,16]{1,2,0:T(8,128)S(1)} all-gather(f32[1,45,16]{1,2,0:T(8,128)S(1)} %convolution_bitcast_fusion), channel_id=1, replica_groups=mesh['cfg'=2,'req'=4,'seq'=32] {'req','seq'}, dimensions={0}, use_global_device_ids=true | all-gather | bytes 371520 | tf_op jit(solution)/shard_map/all_gather | solution.py:91
  362.3 0.5 reshape.193
  364.4 4.6 convolution_convert_fusion
  369.0 0.9 fusion.65
  370.0 0.7 all-gather.8.cloned.1.call-update
  371.3 0.6 copy.43
  372.1 0.6 fusion.63
  372.8 0.6 copy_bitcast_fusion
  373.5 0.9 reshape.189
  374.4 94.2 %all-gather.10.cloned.1.call-done = bf16[4,1024,1152]{2,1,0:T(8,128)(2,1)} async-done(((bf16[4,32,1152]{2,1,0:T(8,128)(2,1)}), bf16[4,1024,1152]{2,1,0:T(8,128)(2,1)}) %all-gather.10.cloned.1.call-update) | async-done | bytes 9437200 | tf_op jit(solution)/shard_map/all_gather | solution.py:124
  468.6 12.7 %copy.26 = bf16[4,1024,1152]{1,2,0:T(8,128)(2,1)} copy(bf16[4,1024,1152]{2,1,0:T(8,128)(2,1)} %all-gather.10.cloned.1.call-done) | data formatting | bytes 18874368 | tf_op jit(solution)/shard_map/all_gather | solution.py:124
  481.3 90.2 %all-gather.8.cloned.1.call-done = bf16[4,1024,1152]{2,1,0:T(8,128)(2,1)} async-done(((bf16[4,32,1152]{2,1,0:T(8,128)(2,1)}), bf16[4,1024,1152]{2,1,0:T(8,128)(2,1)}) %all-gather.8.cloned.1.call-update) | async-done | bytes 9437200 | tf_op jit(solution)/shard_map/all_gather | solution.py:125
  571.4 12.7 %copy.25 = bf16[4,1024,1152]{1,2,0:T(8,128)(2,1)} copy(bf16[4,1024,1152]{2,1,0:T(8,128)(2,1)} %all-gather.8.cloned.1.call-done) | data formatting | bytes 18874368 | tf_op jit(solution)/shard_map/all_gather | solution.py:125
  584.2 5.3 fusion
  589.5 3.2 copy-done.2
  592.7 2.4 fusion.1
  595.1 10.0 %divide_convert_fusion = bf16[4,32,16,72]{3,1,2,0:T(8,128)(2,1)} fusion(bf16[4,1024,16,72]{1,3,2,0:T(8,128)(2,1)} %bitcast.61, f32[4,16,32,1024]{3,2,1,0:T(8,128)} %copy-done.2, f32[4,16,32]{2,1,0:T(8,128)S(1)} %get-tuple-element.32, pred[4,1024]{1,0:T(4,128)(4,1)S(1)} %iota_compare_fusion.3, f32[4,32,16]{1,2,0:T(8,128)S(1)} %bitcast.66), kind=kOutput, calls=%fused_computation.20 | convolution fusion | flops 312770560 | bytes 18141184 | tf_op jit(solution)/shard_map/rhqk,rkhd->rqhd/dot_general | solution.py:140
  605.1 2.0 copy.28
  607.1 1.6 dot_general.40
  608.6 0.8 all-gather.12.cloned.1.call-done
  609.4 2.8 fusion.68
  612.5 1.4 fusion.25
  614.0 71.1 %psum.7 = f32[4]{0:T(128)S(1)} all-reduce(f32[4]{0:T(128)S(1)} %get-tuple-element.3), channel_id=1, replica_groups=mesh['cfg'=2,'req'=4,'seq'=32] {'seq'}, use_global_device_ids=true, to_apply=%region_7.8 | all-reduce | flops 4 | bytes 32 | tf_op jit(solution)/shard_map/psum | solution.py:158
  685.1 1.3 sqrt_bitcast_fusion
  686.3 0.8 select_reduce_fusion.1
  687.2 74.7 %pmax.7 = f32[1,4,16]{2,1,0:T(4,128)} all-reduce(f32[1,4,16]{2,1,0:T(4,128)S(1)} %bitcast.67), channel_id=1, replica_groups=mesh['cfg'=2,'req'=4,'seq'=32] {'seq'}, use_global_device_ids=true, to_apply=%region_9.10 | all-reduce | flops 64 | bytes 512 | tf_op jit(solution)/shard_map/pmax | solution.py:159
  761.9 1.5 fusion.42
  (51 shorter events, 3.3 us)
Async XLA Ops:
  7.2 2.3 copy-start
  7.2 356.2 %copy-start.4 = (f32[4,32,16]{1,2,0:T(8,128)S(1)}, f32[4,32,16]{1,2,0:T(8,128)}, u32[]{:S(2)}) copy-start(f32[4,32,16]{1,2,0:T(8,128)} %param.13) | copy-start | bytes 24580
  7.2 356.2 %copy-start.5 = (bf16[16,1152]{1,0:T(8,128)(2,1)S(1)}, bf16[16,1152]{1,0:T(8,128)(2,1)}, u32[]{:S(2)}) copy-start(bf16[16,1152]{1,0:T(8,128)(2,1)} %param.21) | copy-start | bytes 110596
  7.2 357.1 %all-gather.6.cloned.1.call-start = ((), (), s32[]{:S(2)}) async-start(), calls=%async_computation | async-start | bytes 9953280 | tf_op jit(solution)/shard_map/all_gather | solution.py:114
  7.9 460.7 %all-gather.10.cloned.1.call-start = ((), (), s32[]{:S(2)}) async-start(), calls=%async_computation.2 | async-start | bytes 9732096 | tf_op jit(solution)/shard_map/all_gather | solution.py:124
  364.4 6.9 copy-start.7
  364.4 7.6 copy-start.6
  369.9 201.5 %all-gather.8.cloned.1.call-start = ((), (), s32[]{:S(2)}) async-start(), calls=%async_computation.1 | async-start | bytes 9732096 | tf_op jit(solution)/shard_map/all_gather | solution.py:125
  370.7 238.8 %all-gather.12.cloned.1.call-start = ((), (), s32[]{:S(2)}) async-start(), calls=%async_computation.3 | async-start | bytes 3317760 | tf_op jit(solution)/shard_map/all_gather | solution.py:152
  589.4 3.2 copy-start.2
  589.5 15.6 %copy-start.3 = (f32[4,16,32]{2,1,0:T(8,128)}, f32[4,16,32]{2,1,0:T(8,128)S(1)}, u32[]{:S(2)}) copy-start(f32[4,16,32]{2,1,0:T(8,128)S(1)} %get-tuple-element.32) | copy-start | bytes 24580
  595.1 168.3 %copy-start.1 = (bf16[1152,1152]{1,0:T(8,128)(2,1)S(1)}, bf16[1152,1152]{1,0:T(8,128)(2,1)}, u32[]{:S(2)}) copy-start(bf16[1152,1152]{1,0:T(8,128)(2,1)} %param.19) | copy-start | bytes 7962628
  613.9 148.0 %collective-permute-start = (f32[4,32,32]{1,2,0:T(8,128)S(1)}, f32[4,32,32]{1,2,0:T(8,128)S(1)}, u32[]{:S(2)}, u32[]{:S(2)}) collective-permute-start(f32[4,32,32]{1,2,0:T(8,128)S(1)} %fusion.25), channel_id=1, source_target_pairs={{0,128},{128,0},{1,129},{129,1},{2,130},{130,2},{3,131},{131,3},{4... | collective-permute-start | bytes 49160 | tf_op jit(solution)/shard_map/ppermute | solution.py:19
Sparse Core Ops, SparseCore 0:
  9.8 85.0 all-gather.5
  370.0 98.5 all-gather.9
  471.2 100.1 all-gather.7
  573.1 36.3 all-gather.11
where the time goes:
time: 771 us; the launch traced here: 770 us
  blocking collectives  494 us (64%)
  waiting for transfers between devices  187 us (24%)
  local copies, waits for them, and re-layouts  36.3 us (5%)
  matrix products  28.3 us (4%)
  between operations  14 us (2%)
  other arithmetic  9.52 us (1%)
    all_gather x1, blocking collectives, body(): mod_all = lax.all_gather(mod_part, ('req', 'seq'), axis=1, tiled=True)  349 us
    all_gather x1, waiting for transfers between devices, body(): lax.all_gather(keys_local, 'seq', axis=1, tiled=True)  94.2 us
    all_gather x1, waiting for transfers between devices, body(): lax.all_gather(values_local, 'seq', axis=1, tiled=True)  90.2 us
    pmax x1, blocking collectives, body(): top = lax.pmax(local_top, 'seq')  74.7 us
    psum x1, blocking collectives, body(): total_squares = lax.psum(squares, 'seq')  71.1 us
  transfers between devices with their start and end apart: 5, of which 3 were waited for; matrix products, arithmetic and copies ran while one was open for 8% of the time, Pallas kernels for 0%

commit v1 on v0

--- a/solution.py
+++ b/solution.py
@@ -121,7 +121,9 @@
     values_local = projected[:, 2 * width :].astype(jnp.bfloat16).reshape(req_dev, slot_dev, width)
     inv_root = 1.0 / math.sqrt(head_dim)
     keys_all, values_all = (
-        lax.all_gather(keys_local, "seq", axis=1, tiled=True),
+        jnp.concatenate(
+            lax.all_to_all(jnp.stack([keys_local] * lax.axis_size("seq")), "seq", 0, 0), axis=1
+        ),
         lax.all_gather(values_local, "seq", axis=1, tiled=True),
     )
     keys_heads = keys_all.reshape(req_dev, seq_total, HEADS, head_dim)

time: 771 us -> 847 us (1.099)
  local copies, waits for them, and re-layouts: 36.3 us -> 66.5 us
  starting transfers between devices: 0.43 us -> 13.4 us
  matrix products: 28.3 us -> 40.6 us
  blocking collectives: 494 us -> 504 us
  waiting for transfers between devices: 187 us -> 196 us
    all_to_all x0 -> x1, waiting for transfers between devices: none -> 194 us  [body(): lax.all_to_all(jnp.stack([keys_local] * lax.axis_size('seq')), 'seq', 0, 0)]
    all_gather x1 -> x0, waiting for transfers between devices: 94.2 us -> none  [body(): lax.all_gather(keys_local, 'seq', axis=1, tiled=True)]
    all_gather x1, waiting for transfers between devices: 90.2 us -> 0.01 us  [body(): lax.all_gather(values_local, 'seq', axis=1, tiled=True)]
    another operation x0 -> x2, local copies, waits for them, and re-layouts: none -> 38 us  [the longest x1 33.2 us: body(): keys_heads = keys_all.reshape(req_dev, seq_total, HEADS, head_dim)]
    all_to_all x0 -> x1, starting transfers between devices: none -> 13.2 us  [body(): lax.all_to_all(jnp.stack([keys_local] * lax.axis_size('seq')), 'seq', 0, 0)]
    all_gather x1 -> x0, local copies, waits for them, and re-layouts: 12.7 us -> none  [body(): lax.all_gather(keys_local, 'seq', axis=1, tiled=True)]
    dot_general x1, matrix products: 5.3 us -> 17.8 us  [body(): jnp.einsum('rqhd,rkhd->rhqk', query, keys_heads, preferred_element_type=j...]
    all_gather x1, blocking collectives: 349 us -> 358 us  [body(): mod_all = lax.all_gather(mod_part, ('req', 'seq'), axis=1, tiled=True)]
  transfers between devices with their start and end apart: 5 -> 5, of which waited for: 3 -> 1; matrix products, arithmetic and copies ran while one was open for 8% -> 13% of each run, Pallas kernels for 0% -> 0%
where the time goes in v1:
time: 847 us; the launch traced here: 846 us
  blocking collectives  504 us (60%)
  waiting for transfers between devices  196 us (23%)
  local copies, waits for them, and re-layouts  66.5 us (8%)
  matrix products  40.6 us (5%)
  between operations  14 us (2%)
  starting transfers between devices  13.4 us (2%)
  other arithmetic  12 us (1%)
    all_gather x1, blocking collectives, body(): mod_all = lax.all_gather(mod_part, ('req', 'seq'), axis=1, tiled=True)  358 us
    all_to_all x1, waiting for transfers between devices, body(): lax.all_to_all(jnp.stack([keys_local] * lax.axis_size('seq')), 'seq', 0, 0)  194 us
    pmax x1, blocking collectives, body(): top = lax.pmax(local_top, 'seq')  75 us
    psum x1, blocking collectives, body(): total_squares = lax.psum(squares, 'seq')  70.9 us
    another operation x1, local copies, waits for them, and re-layouts, body(): keys_heads = keys_all.reshape(req_dev, seq_total, HEADS, head_dim)  33.2 us
    dot_general x1, matrix products, body(): jnp.einsum('rqhd,rkhd->rhqk', query, keys_heads, preferred_element_type=j...  17.8 us
  transfers between devices with their start and end apart: 5, of which 1 were waited for; matrix products, arithmetic and copies ran while one was open for 13% of the time, Pallas kernels for 0%

profile of v1, /device:TPU:2, one launch (start us, length us, event | category | flops | bytes accessed | tf_op | source)
XLA Modules:
  0.0 845.9 jit_solution(3711230394826109396)
XLA Ops:
  7.2 0.7 all-gather.5.cloned.1.call-update
  8.0 0.7 convert_element_type.45
  8.7 0.7 broadcast_select_fusion.1
  9.5 1.7 fusion.28
  11.1 2.3 convolution_bitcast_fusion
  13.4 357.6 %all-gather = f32[128,45,16]{1,2,0:T(8,128)S(1)} all-gather(f32[1,45,16]{1,2,0:T(8,128)S(1)} %convolution_bitcast_fusion), channel_id=1, replica_groups=mesh['cfg'=2,'req'=4,'seq'=32] {'req','seq'}, dimensions={0}, use_global_device_ids=true | all-gather | bytes 371520 | tf_op jit(solution)/shard_map/all_gather | solution.py:91
  371.4 0.5 reshape.191
  373.4 4.6 convolution_convert_fusion
  378.0 0.8 fusion.66
  378.8 4.7 stack.3
  383.6 13.2 %all-to-all-start = ((bf16[32,4,32,1152]{3,2,1,0:T(8,128)(2,1)}), bf16[32,4,32,1152]{3,2,1,0:T(8,128)(2,1)}, u32[]{:S(2)}, u32[]{:S(2)}) async-start(bf16[32,4,32,1152]{3,2,1,0:T(8,128)(2,1)} %stack.3), calls=%async_computation | async-start | bytes 18874368 | tf_op jit(solution)/shard_map/all_to_all | solution.py:125
  396.8 0.7 all-gather.9.cloned.1.call-update
  397.8 0.6 fusion.64
  398.4 0.6 copy_bitcast_fusion
  399.1 0.6 copy.48
  399.7 0.9 reshape.188
  400.7 194.3 %all-to-all-done = bf16[32,4,32,1152]{3,2,1,0:T(8,128)(2,1)} async-done(((bf16[32,4,32,1152]{3,2,1,0:T(8,128)(2,1)}), bf16[32,4,32,1152]{3,2,1,0:T(8,128)(2,1)}, u32[]{:S(2)}, u32[]{:S(2)}) %all-to-all-start) | async-done | bytes 9437216 | tf_op jit(solution)/shard_map/all_to_all | solution.py:125
  595.0 8.2 copy.26
  603.3 33.2 %reshape_reshape.3 = bf16[4,1024,16,72]{3,2,1,0:T(8,128)(2,1)} reshape(bf16[4,32,32,1152]{3,2,1,0:T(8,128)(2,1)} %copy.26) | data formatting | bytes 18874368 | tf_op jit(solution)/shard_map/reshape;reshape | solution.py:129
  636.5 12.7 %copy.25 = bf16[4,1024,1152]{1,2,0:T(8,128)(2,1)} copy(bf16[4,1024,1152]{2,1,0:T(8,128)(2,1)} %all-gather.7.cloned.1.call-done) | data formatting | bytes 18874368 | tf_op jit(solution)/shard_map/all_gather | solution.py:127
  649.2 17.8 %fusion.2 = (f32[4,16,32]{2,1,0:T(8,128)S(1)}, f32[4,16,32,1024]{3,2,1,0:T(8,128)}) fusion(pred[4,1024]{1,0:T(4,128)(4,1)S(1)} %iota_compare_fusion.3, bf16[4,1024,16,72]{3,2,1,0:T(8,128)(2,1)} %reshape_reshape.3, bf16[4,32,16,72]{3,2,1,0:T(8,128)(2,1)S(1)} %reshape.188), kind=kOutput, calls=%fused_computation.4 | convolution fusion | flops 308279296 | bytes 18132992 | tf_op jit(solution)/shard_map/rqhd,rkhd->rhqk/dot_general | solution.py:132
  666.9 4.8 fusion.3
  671.8 9.8 %divide_convert_fusion = bf16[4,32,16,72]{3,1,2,0:T(8,128)(2,1)} fusion(bf16[4,1024,16,72]{1,3,2,0:T(8,128)(2,1)} %bitcast.61, f32[4,16,32,1024]{3,2,1,0:T(8,128)} %get-tuple-element.33, f32[4,16,32]{2,1,0:T(8,128)S(1)} %get-tuple-element.32, pred[4,1024]{1,0:T(4,128)(4,1)S(1)} %iota_compare_fusion.3, f32[4,32,16]{1,2,0:T(8,128)S(1)} %bitcast.66), kind=kOutput, calls=%fused_computation.22 | convolution fusion | flops 312770560 | bytes 18141184 | tf_op jit(solution)/shard_map/rhqk,rkhd->rqhd/dot_general | solution.py:142
  681.6 2.1 copy.29
  683.7 1.5 dot_general.40
  685.3 2.8 fusion.69
  688.3 1.4 fusion.26
  689.8 70.9 %psum.7 = f32[4]{0:T(128)S(1)} all-reduce(f32[4]{0:T(128)S(1)} %get-tuple-element.3), channel_id=1, replica_groups=mesh['cfg'=2,'req'=4,'seq'=32] {'seq'}, use_global_device_ids=true, to_apply=%region_7.8 | all-reduce | flops 4 | bytes 32 | tf_op jit(solution)/shard_map/psum | solution.py:160
  760.7 1.3 sqrt_bitcast_fusion
  762.0 0.8 select_reduce_fusion.1
  762.8 75.0 %pmax.7 = f32[1,4,16]{2,1,0:T(4,128)} all-reduce(f32[1,4,16]{2,1,0:T(4,128)S(1)} %bitcast.67), channel_id=1, replica_groups=mesh['cfg'=2,'req'=4,'seq'=32] {'seq'}, use_global_device_ids=true, to_apply=%region_9.10 | all-reduce | flops 64 | bytes 512 | tf_op jit(solution)/shard_map/pmax | solution.py:161
  837.9 1.5 fusion.43
  (50 shorter events, 2.8 us)
Async XLA Ops:
  7.2 2.3 copy-start
  7.2 365.3 %copy-start.3 = (f32[4,32,16]{1,2,0:T(8,128)S(1)}, f32[4,32,16]{1,2,0:T(8,128)}, u32[]{:S(2)}) copy-start(f32[4,32,16]{1,2,0:T(8,128)} %param.13) | copy-start | bytes 24580
  7.2 365.3 %copy-start.4 = (bf16[16,1152]{1,0:T(8,128)(2,1)S(1)}, bf16[16,1152]{1,0:T(8,128)(2,1)}, u32[]{:S(2)}) copy-start(bf16[16,1152]{1,0:T(8,128)(2,1)} %param.21) | copy-start | bytes 110596
  7.2 366.2 %all-gather.5.cloned.1.call-start = ((), (), s32[]{:S(2)}) async-start(), calls=%async_computation.1 | async-start | bytes 9953280 | tf_op jit(solution)/shard_map/all_gather | solution.py:114
  7.9 628.6 %all-gather.7.cloned.1.call-start = ((), (), s32[]{:S(2)}) async-start(), calls=%async_computation.2 | async-start | bytes 9732096 | tf_op jit(solution)/shard_map/all_gather | solution.py:127
  383.5 14.0 %copy-start.6 = (s32[16]{0:T(128)S(1)}, s32[16]{0:T(128)}, u32[]{:S(2)}) copy-start(s32[16]{0:T(128)} %param.17) | copy-start | bytes 196
  383.6 14.1 %copy-start.5 = (s32[16]{0:T(128)S(1)}, s32[16]{0:T(128)}, u32[]{:S(2)}) copy-start(s32[16]{0:T(128)} %param.15) | copy-start | bytes 196
  383.6 211.5 %all-to-all-start = ((bf16[32,4,32,1152]{3,2,1,0:T(8,128)(2,1)}), bf16[32,4,32,1152]{3,2,1,0:T(8,128)(2,1)}, u32[]{:S(2)}, u32[]{:S(2)}) async-start(bf16[32,4,32,1152]{3,2,1,0:T(8,128)(2,1)} %stack.3), calls=%async_computation | async-start | bytes 18874368 | tf_op jit(solution)/shard_map/all_to_all | solution.py:125
  396.8 288.5 %all-gather.9.cloned.1.call-start = ((), (), s32[]{:S(2)}) async-start(), calls=%async_computation.3 | async-start | bytes 3317760 | tf_op jit(solution)/shard_map/all_gather | solution.py:154
  666.9 14.7 %copy-start.2 = (f32[4,16,32]{2,1,0:T(8,128)}, f32[4,16,32]{2,1,0:T(8,128)S(1)}, u32[]{:S(2)}) copy-start(f32[4,16,32]{2,1,0:T(8,128)S(1)} %get-tuple-element.32) | copy-start | bytes 24580
  671.8 167.6 %copy-start.1 = (bf16[1152,1152]{1,0:T(8,128)(2,1)S(1)}, bf16[1152,1152]{1,0:T(8,128)(2,1)}, u32[]{:S(2)}) copy-start(bf16[1152,1152]{1,0:T(8,128)(2,1)} %param.19) | copy-start | bytes 7962628
  689.7 148.1 %collective-permute-start = (f32[4,32,32]{1,2,0:T(8,128)S(1)}, f32[4,32,32]{1,2,0:T(8,128)S(1)}, u32[]{:S(2)}, u32[]{:S(2)}) collective-permute-start(f32[4,32,32]{1,2,0:T(8,128)S(1)} %fusion.26), channel_id=1, source_target_pairs={{0,128},{128,0},{1,129},{129,1},{2,130},{130,2},{3,131},{131,3},{4... | collective-permute-start | bytes 49160 | tf_op jit(solution)/shard_map/ppermute | solution.py:19
Sparse Core Ops, SparseCore 0:
  9.8 85.0 all-gather.4
  378.9 207.6 all-gather.6
  588.4 37.4 all-gather.8
